TPU v7x, 256 devices: a whole 4x4x8 slice. The times are simulated.
256 devices in a mesh: grp: 4 (over y), col: 64 (over x, z, core).
Axes of the slice: x: 4, y: 4, z: 8, core: 2. Of those that a mesh axis runs over, the one named last changes fastest.
Arguments:
- inputs: bfloat16 [24, 256, 8192], P('grp', 'col'), may hold values from -6 to 6
- out_grads: bfloat16 [24, 256, 8192], P('grp', None, 'col'), may hold values from -0.5 to 0.5
- first_moment: float32 [8192, 8192], P(None, 'col'), may hold values from -2 to 2
- second_moment: float32 [8192, 8192], P(None, 'col'), may hold values from 0.01 to 1
- signs_in: int32 [8192], replicated, may hold values from 0 to 1
- signs_out: int32 [8192], replicated, may hold values from 0 to 1
- rows_in: int32 [64], replicated, may hold values from 0 to 8191, as said below
- rows_out: int32 [128], replicated, may hold values from 0 to 8191, as said below
- task_ids: int32 [24], P('grp'), may hold values from 0 to 7
- weights: int32 [24], P('grp'), may hold values from 1 to 4
Outputs:
- prototypes: float32 [8, 64, 128], P('grp', 'col')
Inputs may be any that keep to these rules, and one draw needn't show every extreme that they name: `rows_in`: distinct row numbers. `rows_out`: distinct row numbers.
All inputs are finite; a program needn't handle non-finite values.
Results may differ from a plain program's by a relative error of at most 0.0019.
Values may be sent and summed in bfloat16 or wider, within the bound.
A program may use at most 128 MiB of HBM per device.

v0:
```python
import math
import jax
import jax.numpy as jnp
from jax import lax
from jax.sharding import PartitionSpec as P

PRO_GRP = 2


def hadamard_rows(rows, sign_bits, cols, width):
    both = jnp.bitwise_and(rows[:, None], cols[None, :])
    parity = jnp.zeros(both.shape, jnp.int32)
    for bit in range(int(math.log2(width)) + 1):
        parity = jnp.bitwise_xor(parity, jnp.bitwise_and(jnp.right_shift(both, bit), 1))
    value = (1 - 2 * parity) * (1 - 2 * sign_bits)[None, :]
    return value.astype(jnp.float32)


def body(
    inputs,
    out_grads,
    first_moment,
    second_moment,
    signs_in,
    signs_out,
    rows_in,
    rows_out,
    task_ids,
    weights,
):
    width = first_moment.shape[0]
    n_col = lax.axis_size("col")
    n_grp = lax.axis_size("grp")
    grad = jnp.einsum(
        "etd,etc->edc",
        lax.all_gather(inputs, "col", axis=1, tiled=True),
        out_grads,
        preferred_element_type=jnp.float32,
    )
    first = 0.9 * first_moment[None] + 0.1 * grad
    second = 0.999 * second_moment[None] + 0.001 * grad * grad
    update = (first / (jnp.sqrt(second) + 1e-08)).astype(jnp.bfloat16)
    all_cols = jnp.arange(width, dtype=jnp.int32)
    left = hadamard_rows(rows_in, signs_in, all_cols, width).astype(jnp.bfloat16)
    half = jnp.einsum("rd,edc->erc", left, update, preferred_element_type=jnp.float32)
    right = hadamard_rows(rows_out, signs_out, all_cols, width)
    owned = lax.all_to_all(half, "col", split_axis=1, concat_axis=2, tiled=True)
    sketch = jnp.einsum("erd,kd->erk", owned, right, precision=lax.Precision.HIGHEST)
    entries = sketch.shape[1] * n_col * sketch.shape[2]
    squares = lax.psum(jnp.sum(sketch * sketch, axis=(1, 2)), "col")
    unit = sketch * lax.rsqrt(squares / entries + 1e-06)[:, None, None]
    n_proto = PRO_GRP * n_grp
    protos = jnp.arange(n_proto, dtype=jnp.int32)
    coef = jnp.where(
        task_ids[:, None] == protos[None, :], weights[:, None].astype(jnp.float32), jnp.float32(0.0)
    )
    term = jnp.einsum("ep,erk->prk", coef, unit, precision=lax.Precision.HIGHEST)
    return lax.psum_scatter(term, "grp", scatter_dimension=0, tiled=True)


def solution(mesh):
    placed = (
        P("grp", "col", None),
        P("grp", None, "col"),
        P(None, "col"),
        P(None, "col"),
        P(),
        P(),
        P(),
        P(),
        P("grp"),
        P("grp"),
    )
    return jax.shard_map(
        body, mesh=mesh, in_specs=placed, out_specs=P("grp", "col", None), check_vma=False
    )
```

profile of v0, /device:TPU:0, one launch (start us, length us, event | category | flops | bytes accessed | tf_op | source)
XLA Modules:
  0.0 381.7 jit_solution(12265177928836386276)
XLA Ops:
  6.5 0.0 copy-start
  6.5 0.0 all-gather.2.cloned.1.call-start
  6.5 2.1 copy.12
  8.6 0.0 all-gather.2.cloned.1.call-update
  8.6 0.8 multiply_subtract_fusion.1
  9.4 0.0 copy-start.2
  9.4 7.4 %broadcast_multiply_fusion = (f32[8192,128]{1,0:T(8,128)}, f32[8192,128]{1,0:T(8,128)}) fusion(f32[8192,128]{1,0:T(8,128)} %param.13, f32[8192,128]{1,0:T(8,128)} %param.12), kind=kLoop, calls=%fused_computation.74 | loop fusion | flops 2097152 | bytes 16777216 | tf_op jit(solution)/shard_map/mul | solution.py:41
  16.8 136.3 %all-gather.2.cloned.1.call-done = bf16[6,256,8192]{2,0,1:T(8,128)(2,1)} async-done(((bf16[6,4,8192]{2,0,1:T(8,128)(2,1)}), bf16[6,256,8192]{2,0,1:T(8,128)(2,1)}) %all-gather.2.cloned.1.call-update) | async-done | bytes 25165840 | tf_op jit(solution)/shard_map/all_gather | solution.py:36
  153.1 0.0 copy-done
  153.1 0.0 copy-done.2
  153.1 0.0 copy-start.3
  153.1 0.0 copy-start.6
  153.1 0.0 copy-start.1
  153.1 0.0 copy-start.4
  153.1 56.7 %fusion.76 = f32[6,64,128]{2,1,0:T(8,128)S(1)} fusion(bf16[6,256,128]{2,1,0:T(8,128)(2,1)S(1)} %copy-done, bf16[6,256,8192]{2,0,1:T(8,128)(2,1)} %all-gather.2.cloned.1.call-done, f32[8192,128]{1,0:T(8,128)} %get-tuple-element.7, f32[8192,128]{1,0:T(8,128)} %get-tuple-element.8, s32[8192]{0:T(1024)S(1)} %multiply_subtract_fusion.1, s32[64]{0:T(128)S(1)} %copy-done.2), kind=kOutput, calls=%fused_computation.76 | convolution fusion | flops 4101505024 | bytes 34177280 | tf_op jit(solution)/shard_map/rd,edc->erc/dot_general | solution.py:45
  209.9 0.8 copy.14
  210.7 6.2 %all-to-all-start = ((f32[6,64,128]{2,0,1:T(8,128)}), f32[6,64,128]{2,0,1:T(8,128)S(1)}, u32[]{:S(2)}, u32[]{:S(2)}) async-start(f32[6,64,128]{2,0,1:T(8,128)} %copy.14), calls=%async_computation | async-start | bytes 524288 | tf_op jit(solution)/shard_map/all_to_all | solution.py:47
  216.9 0.0 copy-done.3
  216.9 0.0 copy-done.6
  216.9 0.6 dynamic-slice
  218.1 0.0 copy-done.1
  218.2 0.0 copy-start.5
  218.2 10.7 %all-to-all-done = f32[6,64,128]{2,0,1:T(8,128)S(1)} async-done(((f32[6,64,128]{2,0,1:T(8,128)}), f32[6,64,128]{2,0,1:T(8,128)S(1)}, u32[]{:S(2)}, u32[]{:S(2)}) %all-to-all-start) | async-done | bytes 196640 | tf_op jit(solution)/shard_map/all_to_all | solution.py:47
  228.8 0.0 copy-done.4
  228.8 9.2 %multiply_reduce_fusion = (f32[6]{0:T(128)S(1)}, f32[6,128]{1,0:T(8,128)S(1)}) fusion(s32[8192]{0:T(1024)S(1)} %multiply_subtract_fusion, s32[128]{0:T(128)S(1)} %copy-done.4, f32[6,64,128]{2,0,1:T(8,128)S(1)} %all-to-all-done), kind=kOutput, calls=%fused_computation.99 | convolution fusion | flops 123733496 | bytes 232984 | tf_op jit(solution)/shard_map/erd,kd->erk/dot_general | solution.py:48
  238.0 125.5 %psum.7 = f32[6]{0:T(128)S(1)} all-reduce(f32[6]{0:T(128)S(1)} %get-tuple-element.5), channel_id=1, replica_groups=mesh['grp'=4,'col'=64] {'col'}, use_global_device_ids=true, to_apply=%region_1.0 | all-reduce | flops 6 | bytes 48 | tf_op jit(solution)/shard_map/psum | solution.py:50
  363.5 0.0 copy-done.5
  363.5 0.3 convolution_bitcast_fusion
  363.8 10.5 %all-reduce = f32[8,1,128]{2,0,1:T(8,128)S(1)} all-reduce(f32[8,1,128]{2,0,1:T(8,128)S(1)} %convolution_bitcast_fusion), channel_id=2, replica_groups=mesh['grp'=4,'col'=64] {'grp'}, use_global_device_ids=true, to_apply=%region_2.3.clone | all-reduce | flops 1024 | bytes 8192
  374.3 0.6 constant_dynamic-slice_fusion
  (3 shorter events, 0.0 us)
Async XLA Ops:
  6.5 146.6 %copy-start = (bf16[6,256,128]{2,1,0:T(8,128)(2,1)S(1)}, bf16[6,256,128]{2,1,0:T(8,128)(2,1)}, u32[]{:S(2)}) copy-start(bf16[6,256,128]{2,1,0:T(8,128)(2,1)} %param.11) | copy-start | bytes 1179652
  6.5 146.5 %all-gather.2.cloned.1.call-start = ((), (), s32[]{:S(2)}) async-start(), calls=%async_computation.1 | async-start | bytes 34078720 | tf_op jit(solution)/shard_map/all_gather | solution.py:36
  9.4 143.7 %copy-start.2 = (s32[64]{0:T(128)S(1)}, s32[64]{0:T(128)}, u32[]{:S(2)}) copy-start(s32[64]{0:T(128)} %param.16) | copy-start | bytes 772
  153.1 63.8 %copy-start.3 = (s32[6]{0:T(128)S(1)}, s32[6]{0:T(128)}, u32[]{:S(2)}) copy-start(s32[6]{0:T(128)} %param.19) | copy-start | bytes 76
  153.1 63.8 %copy-start.6 = (u32[256]{0:T(256)S(1)}, u32[256]{0:T(256)}, u32[]{:S(2)}) copy-start(u32[256]{0:T(256)} %constant.13) | copy-start | bytes 3076
  153.1 65.0 %copy-start.1 = (s32[8192]{0:T(1024)S(1)}, s32[8192]{0:T(1024)}, u32[]{:S(2)}) copy-start(s32[8192]{0:T(1024)} %param.15) | copy-start | bytes 98308
  153.1 75.7 %copy-start.4 = (s32[128]{0:T(128)S(1)}, s32[128]{0:T(128)}, u32[]{:S(2)}) copy-start(s32[128]{0:T(128)} %param.17) | copy-start | bytes 1540
  210.7 18.1 %all-to-all-start = ((f32[6,64,128]{2,0,1:T(8,128)}), f32[6,64,128]{2,0,1:T(8,128)S(1)}, u32[]{:S(2)}, u32[]{:S(2)}) async-start(f32[6,64,128]{2,0,1:T(8,128)} %copy.14), calls=%async_computation | async-start | bytes 524288 | tf_op jit(solution)/shard_map/all_to_all | solution.py:47
  218.2 145.4 %copy-start.5 = (s32[6]{0:T(128)S(1)}, s32[6]{0:T(128)}, u32[]{:S(2)}) copy-start(s32[6]{0:T(128)} %param.18) | copy-start | bytes 76
Sparse Core Ops, SparseCore 0:
  10.1 142.9 all-gather.1
where the time goes:
time: 382 us
  waiting for transfers between devices  147 us (38%)
  blocking collectives  136 us (36%)
  matrix products  66.2 us (17%)
  between operations  14.2 us (4%)
  other arithmetic  8.18 us (2%)
  starting transfers between devices  6.16 us (2%)
  local copies, waits for them, and re-layouts  4.09 us (1%)
    all_gather x1, waiting for transfers between devices, body(): lax.all_gather(inputs, 'col', axis=1, tiled=True)  136 us
    psum x1, blocking collectives, body(): squares = lax.psum(jnp.sum(sketch * sketch, axis=(1, 2)), 'col')  126 us
    dot_general x1, matrix products, body(): jnp.einsum('rd,edc->erc', left, update, preferred_element_type=jnp.float32)  56.7 us
    all_to_all x1, waiting for transfers between devices, body(): owned = lax.all_to_all(half, 'col', split_axis=1, concat_axis=2, tiled=True)  10.7 us
    unnamed x1, blocking collectives  10.5 us
    dot_general x1, matrix products, body(): jnp.einsum('erd,kd->erk', owned, right, precision=lax.Precision.HIGHEST)  9.18 us
  transfers between devices with their start and end apart: 2, of which 2 were waited for; matrix products, arithmetic and copies ran while one was open for 2% of the time, Pallas kernels for 0%

commit v1 on v0

--- a/solution.py
+++ b/solution.py
@@ -33,7 +33,9 @@
     n_grp = lax.axis_size("grp")
     grad = jnp.einsum(
         "etd,etc->edc",
-        lax.all_gather(inputs, "col", axis=1, tiled=True),
+        jnp.concatenate(
+            lax.all_to_all(jnp.stack([inputs] * lax.axis_size("col")), "col", 0, 0), axis=1
+        ),
         out_grads,
         preferred_element_type=jnp.float32,
     )

time: 382 us -> 819 us (2.14)
  waiting for transfers between devices: 147 us -> 549 us
  local copies, waits for them, and re-layouts: 4.09 us -> 68.9 us
  matrix products: 66.2 us -> 35.5 us
  between operations: 14.2 us -> 0.8 us
  starting transfers between devices: 6.16 us -> 19.5 us
    all_to_all x0 -> x1, waiting for transfers between devices: none -> 539 us  [body(): lax.all_to_all(jnp.stack([inputs] * lax.axis_size('col')), 'col', 0, 0)]
    all_gather x1 -> x0, waiting for transfers between devices: 136 us -> none  [body(): lax.all_gather(inputs, 'col', axis=1, tiled=True)]
    reshape x0 -> x2, local copies, waits for them, and re-layouts: none -> 52.4 us  [body(): jnp.concatenate(lax.all_to_all(jnp.stack([inputs] * lax.axis_size('col'))...]
    dot_general x1, matrix products: 56.7 us -> 26 us  [body(): jnp.einsum('rd,edc->erc', left, update, preferred_element_type=jnp.float32)]
    another operation x0 -> x1, local copies, waits for them, and re-layouts: none -> 14.5 us  [body(): jnp.stack([inputs] * lax.axis_size('col'))]
    all_to_all x0 -> x1, starting transfers between devices: none -> 10.6 us  [body(): lax.all_to_all(jnp.stack([inputs] * lax.axis_size('col')), 'col', 0, 0)]
  transfers between devices with their start and end apart: 2 -> 2, of which waited for: 2 -> 2; matrix products, arithmetic and copies ran while one was open for 2% -> 1% of each run, Pallas kernels for 0% -> 0%
where the time goes in v1:
time: 819 us; the launch traced here: 817 us
  waiting for transfers between devices  549 us (67%)
  blocking collectives  136 us (17%)
  local copies, waits for them, and re-layouts  68.9 us (8%)
  matrix products  35.5 us (4%)
  starting transfers between devices  19.5 us (2%)
    all_to_all x1, waiting for transfers between devices, body(): lax.all_to_all(jnp.stack([inputs] * lax.axis_size('col')), 'col', 0, 0)  539 us
    psum x1, blocking collectives, body(): squares = lax.psum(jnp.sum(sketch * sketch, axis=(1, 2)), 'col')  126 us
    reshape x2, local copies, waits for them, and re-layouts, body(): jnp.concatenate(lax.all_to_all(jnp.stack([inputs] * lax.axis_size('col'))...  52.4 us
    dot_general x1, matrix products, body(): jnp.einsum('rd,edc->erc', left, update, preferred_element_type=jnp.float32)  26 us
  transfers between devices with their start and end apart: 2, of which 2 were waited for; matrix products, arithmetic and copies ran while one was open for 1% of the time, Pallas kernels for 0%

profile of v1, /device:TPU:0, one launch (start us, length us, event | category | flops | bytes accessed | tf_op | source)
XLA Modules:
  0.0 817.5 jit_solution(8479183445325976991)
XLA Ops:
  0.0 0.0 copy-start
  0.0 14.5 %stack.2 = bf16[64,6,4,8192]{3,2,1,0:T(4,128)(2,1)} broadcast(bf16[6,4,8192]{2,1,0:T(4,128)(2,1)} %param.10), dimensions={1,2,3} | broadcast | bytes 25559040 | tf_op jit(solution)/shard_map/stack | solution.py:37
  14.5 0.0 copy-start.2
  14.5 10.6 %all-to-all-start = ((bf16[64,6,4,8192]{3,2,1,0:T(4,128)(2,1)}), bf16[64,6,4,8192]{3,2,1,0:T(4,128)(2,1)}, u32[]{:S(2)}, u32[]{:S(2)}) async-start(bf16[64,6,4,8192]{3,2,1,0:T(4,128)(2,1)} %stack.2), calls=%async_computation | async-start | bytes 50331648 | tf_op jit(solution)/shard_map/all_to_all | solution.py:37
  25.1 0.0 copy-done.2
  25.2 7.4 broadcast_multiply_fusion
  32.6 538.6 %all-to-all-done = bf16[64,6,4,8192]{3,2,1,0:T(4,128)(2,1)} async-done(((bf16[64,6,4,8192]{3,2,1,0:T(4,128)(2,1)}), bf16[64,6,4,8192]{3,2,1,0:T(4,128)(2,1)}, u32[]{:S(2)}, u32[]{:S(2)}) %all-to-all-start) | async-done | bytes 25165856 | tf_op jit(solution)/shard_map/all_to_all | solution.py:37
  571.2 17.6 %copy.15 = bf16[6,64,4,8192]{3,2,1,0:T(4,128)(2,1)} copy(bf16[6,64,4,8192]{3,2,0,1:T(4,128)(2,1)} %bitcast) | data formatting | bytes 50331648 | tf_op jit(solution)/shard_map/reshape | solution.py:36
  588.8 0.0 copy-start.4
  588.8 34.8 %reshape.37 = bf16[6,256,8192]{2,1,0:T(8,128)(2,1)} reshape(bf16[6,64,4,8192]{3,2,1,0:T(4,128)(2,1)} %copy.15) | data formatting | bytes 50331648 | tf_op jit(solution)/shard_map/reshape | solution.py:36
  623.6 0.0 copy-done
  623.6 0.0 copy-done.4
  623.6 0.0 copy-start.5
  623.6 0.0 copy-start.8
  623.6 0.0 copy-start.3
  623.6 0.0 copy-start.6
  623.6 26.0 %fusion.71 = f32[6,64,128]{2,1,0:T(8,128)S(1)} fusion(f32[8192,128]{1,0:T(8,128)} %get-tuple-element.7, f32[8192,128]{1,0:T(8,128)} %get-tuple-element.8, s32[8192]{0:T(1024)S(1)} %multiply_subtract_fusion.1, s32[64]{0:T(128)S(1)} %copy-done.4, bf16[6,256,8192]{2,1,0:T(8,128)(2,1)} %reshape.37, bf16[6,256,128]{2,1,0:T(8,128)(2,1)S(1)} %copy-done), kind=kOutput, calls=%fused_computation.74 | convolution fusion | flops 4101505024 | bytes 34177280 | tf_op jit(solution)/shard_map/rd,edc->erc/dot_general | solution.py:47
  649.6 0.8 copy.17
  650.5 8.9 %all-to-all-start.1 = ((f32[6,64,128]{2,0,1:T(8,128)}), f32[6,64,128]{2,0,1:T(8,128)S(1)}, u32[]{:S(2)}, u32[]{:S(2)}) async-start(f32[6,64,128]{2,0,1:T(8,128)} %copy.17), calls=%async_computation.1 | async-start | bytes 524288 | tf_op jit(solution)/shard_map/all_to_all | solution.py:49
  659.4 0.0 copy-done.5
  659.4 0.0 copy-done.8
  659.5 0.6 dynamic-slice
  660.7 0.0 copy-done.3
  660.7 0.0 copy-start.7
  660.7 10.5 %all-to-all-done.1 = f32[6,64,128]{2,0,1:T(8,128)S(1)} async-done(((f32[6,64,128]{2,0,1:T(8,128)}), f32[6,64,128]{2,0,1:T(8,128)S(1)}, u32[]{:S(2)}, u32[]{:S(2)}) %all-to-all-start.1) | async-done | bytes 196640 | tf_op jit(solution)/shard_map/all_to_all | solution.py:49
  671.2 0.0 copy-done.6
  671.2 0.0 copy-start.1
  671.2 9.2 %multiply_reduce_fusion = (f32[6]{0:T(128)S(1)}, f32[6,128]{1,0:T(8,128)S(1)}) fusion(s32[8192]{0:T(1024)S(1)} %multiply_subtract_fusion, s32[128]{0:T(128)S(1)} %copy-done.6, f32[6,64,128]{2,0,1:T(8,128)S(1)} %all-to-all-done.1), kind=kOutput, calls=%fused_computation.97 | convolution fusion | flops 123733496 | bytes 232984 | tf_op jit(solution)/shard_map/erd,kd->erk/dot_general | solution.py:50
  680.4 125.5 %psum.7 = f32[6]{0:T(128)S(1)} all-reduce(f32[6]{0:T(128)S(1)} %get-tuple-element.5), channel_id=1, replica_groups=mesh['grp'=4,'col'=64] {'col'}, use_global_device_ids=true, to_apply=%region_1.0 | all-reduce | flops 6 | bytes 48 | tf_op jit(solution)/shard_map/psum | solution.py:52
  805.9 0.0 copy-done.7
  805.9 0.3 convolution_bitcast_fusion
  806.2 10.7 %all-reduce = f32[8,1,128]{2,0,1:T(8,128)S(1)} all-reduce(f32[8,1,128]{2,0,1:T(8,128)S(1)} %convolution_bitcast_fusion), channel_id=2, replica_groups=mesh['grp'=4,'col'=64] {'grp'}, use_global_device_ids=true, to_apply=%region_2.3.clone | all-reduce | flops 1024 | bytes 8192
  816.9 0.6 constant_dynamic-slice_fusion
  817.5 0.0 copy-done.1
  (4 shorter events, 0.0 us)
Async XLA Ops:
  0.0 623.6 %copy-start = (bf16[6,256,128]{2,1,0:T(8,128)(2,1)S(1)}, bf16[6,256,128]{2,1,0:T(8,128)(2,1)}, u32[]{:S(2)}) copy-start(bf16[6,256,128]{2,1,0:T(8,128)(2,1)} %param.11) | copy-start | bytes 1179652
  14.5 10.6 %copy-start.2 = (s32[8192]{0:T(1024)S(1)}, s32[8192]{0:T(1024)}, u32[]{:S(2)}) copy-start(s32[8192]{0:T(1024)} %param.14) | copy-start | bytes 98308
  14.5 556.7 %all-to-all-start = ((bf16[64,6,4,8192]{3,2,1,0:T(4,128)(2,1)}), bf16[64,6,4,8192]{3,2,1,0:T(4,128)(2,1)}, u32[]{:S(2)}, u32[]{:S(2)}) async-start(bf16[64,6,4,8192]{3,2,1,0:T(4,128)(2,1)} %stack.2), calls=%async_computation | async-start | bytes 50331648 | tf_op jit(solution)/shard_map/all_to_all | solution.py:37
  588.8 34.8 %copy-start.4 = (s32[64]{0:T(128)S(1)}, s32[64]{0:T(128)}, u32[]{:S(2)}) copy-start(s32[64]{0:T(128)} %param.16) | copy-start | bytes 772
  623.6 35.8 %copy-start.5 = (s32[6]{0:T(128)S(1)}, s32[6]{0:T(128)}, u32[]{:S(2)}) copy-start(s32[6]{0:T(128)} %param.19) | copy-start | bytes 76
  623.6 35.9 %copy-start.8 = (u32[256]{0:T(256)S(1)}, u32[256]{0:T(256)}, u32[]{:S(2)}) copy-start(u32[256]{0:T(256)} %constant.13) | copy-start | bytes 3076
  623.6 37.1 %copy-start.3 = (s32[8192]{0:T(1024)S(1)}, s32[8192]{0:T(1024)}, u32[]{:S(2)}) copy-start(s32[8192]{0:T(1024)} %param.15) | copy-start | bytes 98308
  623.6 47.6 %copy-start.6 = (s32[128]{0:T(128)S(1)}, s32[128]{0:T(128)}, u32[]{:S(2)}) copy-start(s32[128]{0:T(128)} %param.17) | copy-start | bytes 1540
  650.5 20.7 %all-to-all-start.1 = ((f32[6,64,128]{2,0,1:T(8,128)}), f32[6,64,128]{2,0,1:T(8,128)S(1)}, u32[]{:S(2)}, u32[]{:S(2)}) async-start(f32[6,64,128]{2,0,1:T(8,128)} %copy.17), calls=%async_computation.1 | async-start | bytes 524288 | tf_op jit(solution)/shard_map/all_to_all | solution.py:49
  660.7 145.2 %copy-start.7 = (s32[6]{0:T(128)S(1)}, s32[6]{0:T(128)}, u32[]{:S(2)}) copy-start(s32[6]{0:T(128)} %param.18) | copy-start | bytes 76
  671.2 146.3 %copy-start.1 = (bf16[6,256,128]{2,1,0:T(8,128)(2,1)S(1)}, bf16[6,256,128]{2,1,0:T(8,128)(2,1)}, u32[]{:S(2)}) copy-start(bf16[6,256,128]{2,1,0:T(8,128)(2,1)} %param.11) | copy-start | bytes 1179652
